TPU v7x, 256 devices: a whole 4x4x8 slice. The times are simulated.
256 devices in a mesh: kx: 32 (over z, x), ky: 8 (over y, core).
Axes of the slice: x: 4, y: 4, z: 8, core: 2. Of those that a mesh axis runs over, the one named last changes fastest.
Arguments:
- slip_rate: float32 [3, 2048, 2048], P(None, ('kx', 'ky')), may hold values from -6 to 6
- slip_field: float32 [3, 2048, 2048], P(None, ('kx', 'ky')), may hold values from -6 to 6
- prestress: float32 [3, 2048, 2048], P(None, ('kx', 'ky')), may hold values from -6 to 6
- history: bfloat16 [6, 3, 2, 2048, 2048], P(None, None, None, ('kx', 'ky')), may hold values from -6 to 6
- kernel: float32 [8, 8, 3], replicated, may hold values from -3 to 3
- band_len: int32 [8], replicated, may hold values from 2 to 8, as said below
- mode_band: int32 [2048, 2048], P(('kx', 'ky')), may hold values from 0 to 7
Outputs:
- new_rate: float32 [3, 2048, 2048], P(None, ('kx', 'ky'))
- new_slip: float32 [3, 2048, 2048], P(None, ('kx', 'ky'))
Inputs may be any that keep to these rules, and one draw needn't show every extreme that they name: `band_len`: entry 0 equals 8; every other entry lies between 2 and 4.
All inputs are finite; a program needn't handle non-finite values.
Results may differ from a plain program's by a relative error of at most 0.0003.
Values sent between devices are 32-bit elements; how exact they have to be, the bound alone decides.
A program may use at most 128 MiB of HBM per device.

v0:
```python
import functools

import jax
import jax.numpy as jnp
import numpy as np
from jax import lax
from jax.experimental import pallas as pl
from jax.experimental.pallas import tpu as pltpu
from jax.sharding import PartitionSpec as P

MESH = pl.DeviceIdType.MESH
N = 2048
DEV = 256
SLOTS = 5
BANDS = 8
LAGS = 8
F32 = jnp.float32
BF16 = jnp.bfloat16


def split(table):
    table = np.asarray(table, np.float64)
    high = table.astype(np.float32).astype(jnp.bfloat16)
    low = (table - high.astype(np.float64)).astype(np.float32).astype(jnp.bfloat16)
    return np.stack([np.asarray(high), np.asarray(low)])


def lane(slot, comp, at):
    return slot * 24 + comp * 8 + at


@functools.cache
def tables():
    scale = 1.0 / np.sqrt(N)
    k2, n2 = np.arange(256)[:, None], np.arange(512)[None, :]
    angle = 2 * np.pi / 512 * (k2 * n2 % 512)
    y_table = split(np.concatenate([np.cos(angle), np.sin(angle)], 1) * scale)
    k1, s = np.arange(256)[:, None], np.arange(256)[None, :]
    angle = 2 * np.pi / 256 * (k1 * s % 256)
    x_table = split(np.concatenate([np.cos(angle), np.sin(angle)], 1) * scale)
    slots = np.arange(8)[:, None]
    angle = 2 * np.pi / N * (slots * n2 % N)
    y_twist = np.stack([np.cos(angle), np.sin(angle)]).astype(np.float32)
    x_twist = np.zeros((2, 256, 128), np.float32)
    eight = np.arange(8)
    for slot in range(SLOTS):
        for comp in range(3):
            at = lane(slot, comp, 0)
            angle = 2 * np.pi / N * (np.arange(256)[:, None] * eight[None, :])
            x_twist[0, :, at : at + 8] = np.cos(angle)
            x_twist[1, :, at : at + 8] = np.sin(angle)
    angle = 2 * np.pi / 8 * (eight[:, None] * eight[None, :] % 8)
    cos8, sin8 = np.cos(angle), np.sin(angle)
    forward = np.zeros((256, 256))
    inverse = np.zeros((256, 256))
    for slot in range(SLOTS):
        for comp in range(3):
            at = lane(slot, comp, 0)
            re, im = slice(at, at + 8), slice(128 + at, 128 + at + 8)
            forward[re, re], forward[im, re] = cos8, sin8
            forward[re, im], forward[im, im] = -sin8, cos8
            inverse[re, re], inverse[im, re] = cos8, -sin8
            inverse[re, im], inverse[im, im] = sin8, cos8
    eights = np.stack([split(forward), split(inverse)])
    own_rows = [{0: 0, 1: 1, 2: 2, 3: 3}, {0: 4, 1: 3, 2: 2, 3: 1, 4: 0}]
    sent_rows = [{0: 4, 1: 5, 2: 6, 3: 7}, {1: 7, 2: 6, 3: 5}]
    past = np.zeros((2, 384, 512))
    for half in range(2):
        for block, rows in enumerate((own_rows[half], sent_rows[half])):
            for slot, row in rows.items():
                for comp in range(3):
                    out = block * 256 + lane(slot, comp, 0)
                    re, im = slice(out, out + 8), slice(out + 128, out + 136)
                    for mode in range(8):
                        in_re = ((comp * 2 + 0) * 8 + mode) * 8 + row
                        in_im = ((comp * 2 + 1) * 8 + mode) * 8 + row
                        past[half, in_re, re] = cos8[mode]
                        past[half, in_im, re] = -sin8[mode]
                        past[half, in_re, im] = sin8[mode]
                        past[half, in_im, im] = cos8[mode]
    past = np.stack([split(past[0]), split(past[1])])
    picks = np.zeros((2, 3, 128, 128), np.float32)
    missing = np.full((2, 2, 8, 128), 8.0, np.float32)
    plain = [{slot: (0, slot) for slot in range(4)}, {slot: (1, 4 + slot) for slot in range(4)}]
    turned = [{slot: (1, 8 - slot) for slot in (1, 2, 3)}, {slot: (0, 4 - slot) for slot in range(5)}]
    for half in range(2):
        for kind, (which, source) in enumerate(
            ((plain, eight), (turned, 7 - eight), (turned, (8 - eight) % 8))
        ):
            for slot, (block, row) in which[half].items():
                for comp in range(3):
                    for mode in range(8):
                        out = lane(slot, comp, mode)
                        picks[half, kind, (block * 8 + source[mode]) * 8 + row, out] = 1.0
                        missing[half, min(kind, 1), :, out] = 0.0
    picks = picks.astype(jnp.bfloat16)
    turn = np.zeros((256, 256), np.float32)
    turn[np.arange(256), (256 - np.arange(256)) % 256] = 1.0
    turn = turn.astype(jnp.bfloat16)
    return y_table, x_table, y_twist, x_twist, eights, past, picks, missing, turn


def halves(value):
    high = value.astype(BF16)
    low = (value - high.astype(F32)).astype(BF16)
    return high, low


NN = (((1,), (0,)), ((), ()))
NT = (((1,), (1,)), ((), ()))


def product(left, right, dims=NN):
    (left_high, left_low), (right_high, right_low) = left, right
    dot = functools.partial(lax.dot_general, dimension_numbers=dims, preferred_element_type=F32)
    return dot(left_high, right_high) + (dot(left_high, right_low) + dot(left_low, right_high))


def softplus(value):
    return jnp.maximum(value, 0.0) + jnp.log1p(jnp.exp(-jnp.abs(value)))


def block_of(device):
    return 2 * device + (device // 128) * (511 - 4 * device)


def body(
    slip_rate, slip_field, prestress, history, mode_band,
    y_table, x_table, y_twist, x_twist, eights, past, picks, missing, turn,
    kern, band_len,
    new_rate, new_slip,
    send, recv, stacked, bands, given, taken, partner_band,
    send_sem, recv_sem, pair_send, pair_recv, own_sem,
):
    kx, ky = lax.axis_index("kx"), lax.axis_index("ky")
    me = kx * 8 + ky
    half = me // 128
    mine = block_of(me)
    partner = 255 - me
    partner_id = (partner // 8, lax.rem(partner, 8))

    barrier = pltpu.get_barrier_semaphore()

    def greet(step, carry):
        other = lax.rem(me + step, DEV)
        pl.semaphore_signal(
            barrier, inc=1, device_id=(other // 8, lax.rem(other, 8)), device_id_type=MESH
        )
        return carry

    lax.fori_loop(1, DEV, greet, 0)

    def exchange(turn_at, forward):
        def one(device):
            if forward:
                source, target = send.at[turn_at, block_of(device)], recv.at[turn_at, me]
            else:
                source, target = send.at[turn_at, device], recv.at[turn_at, mine]
            pltpu.make_async_remote_copy(
                source, target, send_sem.at[turn_at], recv_sem.at[turn_at],
                device_id=(device // 8, lax.rem(device, 8)), device_id_type=MESH,
            ).start()

        one(lax.rem(me + 128, DEV))

        def two(step, carry):
            one(lax.rem(me + 128 + step, DEV))
            one(lax.rem(me + 128 - step, DEV))
            return carry

        lax.fori_loop(1, 128, two, 0)
        if forward:
            source, target = send.at[turn_at, mine], recv.at[turn_at, me]
        else:
            source, target = send.at[turn_at, me], recv.at[turn_at, mine]
        pltpu.make_async_copy(source, target, recv_sem.at[turn_at]).start()

    def arrive(turn_at):
        whole = recv.at[turn_at]
        pltpu.make_async_copy(whole, whole, recv_sem.at[turn_at]).wait()
        gone = send.at[turn_at, pl.ds(0, DEV - 1)]
        pltpu.make_async_copy(gone, gone, send_sem.at[turn_at]).wait()

    def put(turn_at, re, im):
        send[turn_at, :, 0, :] = re
        send[turn_at, :, 1, :] = im

    def y_forward(field):
        cos, sin = y_twist[0], y_twist[1]
        re_rows, im_rows = [[] for _ in range(SLOTS)], [[] for _ in range(SLOTS)]
        for comp in range(3):
            part = [field[comp][:, 512 * n : 512 * (n + 1)] for n in range(4)]
            even, odd = part[0] + part[2], part[1] + part[3]
            left, right = part[0] - part[2], part[1] - part[3]
            pairs = [(even + odd, None), (left, -right), (even - odd, None), (left, right), (even + odd, None)]
            for slot, (re, im) in enumerate(pairs):
                c, s = cos[slot : slot + 1], sin[slot : slot + 1]
                if slot == 0:
                    re_rows[slot].append(re)
                    im_rows[slot].append(jnp.zeros_like(re))
                elif im is None:
                    re_rows[slot].append(re * c)
                    im_rows[slot].append(-(re * s))
                else:
                    re_rows[slot].append(re * c + im * s)
                    im_rows[slot].append(im * c - re * s)
        pad = jnp.zeros((8, 512), F32)
        re = jnp.concatenate(sum(re_rows, []) + [pad], 0)
        im = jnp.concatenate(sum(im_rows, []) + [pad], 0)
        re_high, re_low = halves(re)
        im_high, im_low = halves(im)

        def arrange(r, i):
            return jnp.concatenate([jnp.concatenate([r, i], 1), jnp.concatenate([i, -r], 1)], 0)

        out = product(
            (y_table[0], y_table[1]), (arrange(re_high, im_high), arrange(re_low, im_low)), NT
        )
        return out[:, :128], out[:, 128:]

    def y_inverse(turn_at):
        re = halves(recv[turn_at, :, 0, :].T)
        im = halves(recv[turn_at, :, 1, :].T)

        def arrange(r, i):
            return jnp.concatenate([jnp.concatenate([r, -i], 1), jnp.concatenate([i, r], 1)], 0)

        def tall(n):
            return jnp.concatenate([y_table[n, :, :512], y_table[n, :, 512:]], 0)

        out = product((arrange(re[0], im[0]), arrange(re[1], im[1])), (tall(0), tall(1)))
        cos, sin = y_twist[0], y_twist[1]

        def turned(slot, comp, want_im):
            a = out[lane(slot, comp, 0) : lane(slot, comp, 8)]
            if slot == 0:
                return a, None
            b = out[128 + lane(slot, comp, 0) : 128 + lane(slot, comp, 8)]
            c, s = cos[slot : slot + 1], sin[slot : slot + 1]
            return a * c - b * s, (b * c + a * s) if want_im else None

        field = []
        for comp in range(3):
            base = turned(0, comp, False)[0] + turned(4, comp, False)[0]
            one_re, one_im = turned(1, comp, True)
            two_re, _ = turned(2, comp, False)
            three_re, three_im = turned(3, comp, True)
            up, down = base + two_re, base - two_re
            re_sum, im_dif = one_re + three_re, one_im - three_im
            field.append([up + re_sum, down - im_dif, up - re_sum, down + im_dif])
        return field

    def x_transform(re, im, sign):
        re_high, re_low = halves(re)
        im_high, im_low = halves(im)

        def arrange(r, i):
            if sign < 0:
                return jnp.concatenate([jnp.concatenate([r, i], 1), jnp.concatenate([i, -r], 1)], 0)
            return jnp.concatenate([jnp.concatenate([r, i], 1), jnp.concatenate([-i, r], 1)], 0)

        out = product(
            (x_table[0], x_table[1]), (arrange(re_high, im_high), arrange(re_low, im_low))
        )
        return out[:, :128], out[:, 128:]

    def twist(re, im, sign):
        cos, sin = x_twist[0], x_twist[1]
        if sign < 0:
            return re * cos + im * sin, im * cos - re * sin
        return re * cos - im * sin, im * cos + re * sin

    def x_forward(turn_at):
        re, im = x_transform(recv[turn_at, :, 0, :], recv[turn_at, :, 1, :], -1)
        re, im = twist(re, im, -1)
        out = product(halves(jnp.concatenate([re, im], 1)), (eights[0, 0], eights[0, 1]))
        return out[:, :128], out[:, 128:]

    def x_inverse(re, im):
        out = product(halves(jnp.concatenate([re, im], 1)), (eights[1, 0], eights[1, 1]))
        re, im = twist(out[:, :128], out[:, 128:], 1)
        return x_transform(re, im, 1)

    put(0, *y_forward([slip_rate[comp] for comp in range(3)]))
    pl.semaphore_wait(barrier, DEV - 1)
    exchange(0, True)
    band_copy = pltpu.make_async_remote_copy(
        mode_band, partner_band, pair_send.at[0], pair_recv.at[0],
        device_id=partner_id, device_id_type=MESH,
    )
    band_copy.start()

    def live(band, lag, comp):
        kept = (band_len[band] > lag).astype(F32)
        return kern[(band * LAGS + lag) * 3 + comp] * kept

    effective = {
        (band, lag, comp): live(band, lag, comp)
        for lag in (0, 1, 2, 3) for comp in range(3) for band in range(BANDS)
    }
    effective.update({(0, lag, comp): live(0, lag, comp) for lag in range(4, LAGS) for comp in range(3)})

    def gather(mode, carry):
        at = pl.multiple_of(mode * 256, 256)
        band = mode_band[:, pl.ds(at, 256)]
        chosen = [band == b for b in range(BANDS)]
        for comp in range(3):
            total = [jnp.zeros((8, 256), F32), jnp.zeros((8, 256), F32)]
            for lag in range(2, LAGS):
                weight = jnp.zeros((8, 256), F32)
                for b in range(BANDS if lag < 4 else 1):
                    weight = jnp.where(chosen[b], effective[b, lag, comp], weight)
                for part in range(2):
                    source = history[lag - 2, comp, part, :, pl.ds(at, 256)].astype(F32)
                    total[part] = total[part] + weight * source
            for part in range(2):
                row = pl.multiple_of(((comp * 2 + part) * 8 + mode) * 8, 8)
                stacked[pl.ds(row, 8), :] = total[part]
        row = pl.multiple_of(mode * 8, 8)
        bands[pl.ds(row, 8), :] = band.astype(F32)
        return carry

    lax.fori_loop(0, 8, gather, 0)
    flat = halves(stacked[...].T)
    out = product(flat, (past[half, 0], past[half, 1]))
    given_re, given_im = x_transform(*twist(out[:, 256:384], out[:, 384:], 1), 1)
    given[0] = given_re
    given[1] = given_im
    given_copy = pltpu.make_async_remote_copy(
        given, taken, pair_send.at[1], pair_recv.at[1],
        device_id=partner_id, device_id_type=MESH,
    )
    given_copy.start()
    own_re, own_im = x_transform(*twist(out[:, :128], out[:, 128:256], 1), 1)

    band_copy.wait()
    for mode in range(8):
        bands[64 + mode * 8 : 72 + mode * 8, :] = partner_band[:, mode * 256 : (mode + 1) * 256].astype(F32)
    plain = bands[...].T.astype(BF16)
    dot = functools.partial(lax.dot_general, dimension_numbers=NN, preferred_element_type=F32)
    turned = dot(turn[...], plain).astype(BF16)
    first_row = lax.broadcasted_iota(jnp.int32, (256, 128), 0) == 0
    plain_band = dot(plain, picks[half, 0]) + missing[half, 0, 0:1]
    turned_band = (
        jnp.where(first_row, dot(turned, picks[half, 2]), dot(turned, picks[half, 1]))
        + missing[half, 1, 0:1]
    )
    lane_at = lax.broadcasted_iota(jnp.int32, (1, 128), 1)
    lane_comp = lax.rem(lane_at // 8, 3)
    weight = [jnp.zeros((256, 128), F32) for _ in range(2)]
    for which in (plain_band, turned_band):
        chosen = [jnp.zeros((256, 128), F32) for _ in range(2)]
        for b in range(BANDS):
            hit = which == float(b)
            for lag in range(2):
                value = jnp.where(
                    lane_comp == 0, effective[b, lag, 0],
                    jnp.where(lane_comp == 1, effective[b, lag, 1], effective[b, lag, 2]),
                )
                chosen[lag] = jnp.where(hit, value, chosen[lag])
        weight = [weight[lag] + chosen[lag] for lag in range(2)]
    first_weight = weight[0] + weight[1]
    now_weight = weight[1] + 0.5 * weight[0]
    tried_weight = 0.5 * weight[0]

    given_copy.wait()
    sign = 1.0 - 2.0 * half.astype(F32)
    held_re = own_re + taken[0]
    held_im = sign * (own_im - taken[1])

    slip = [slip_field[comp] for comp in range(2)]
    worn = jnp.sqrt(slip[0] * slip[0] + slip[1] * slip[1] + 1.0) - 1.0
    coeff = 0.35 + 0.35 * jnp.exp(worn * -2.0)

    def slide(field, write):
        rates = [[], [], []]
        for n in range(4):
            part = slice(512 * n, 512 * (n + 1))
            s = [prestress[comp, :, part] + field[comp][n] for comp in range(3)]
            strength = coeff[:, part] * softplus(-s[2])
            magnitude = jnp.sqrt(s[0] * s[0] + s[1] * s[1] + 1.0)
            ratio = softplus(magnitude - strength) / magnitude
            for comp, value in enumerate((ratio * s[0], ratio * s[1], softplus(s[2]))):
                if write:
                    new_rate[comp, :, part] = value
                    new_slip[comp, :, part] = slip_field[comp, :, part] + 0.25 * (
                        slip_rate[comp, :, part] + value
                    )
                rates[comp].append(value)
        return [jnp.concatenate(rate, 1) for rate in rates]

    arrive(0)
    now_re, now_im = x_forward(0)
    re, im = x_inverse(now_re * first_weight, now_im * first_weight)
    put(1, re + held_re, im + held_im)
    exchange(1, False)
    re, im = x_inverse(now_re * now_weight, now_im * now_weight)
    given[0] = re + held_re
    given[1] = im + held_im
    arrive(1)
    first = slide(y_inverse(1), False)

    put(2, *y_forward(first))
    exchange(2, True)
    arrive(2)
    re, im = x_forward(2)
    re, im = x_inverse(re * tried_weight, im * tried_weight)
    put(3, re + given[0], im + given[1])
    exchange(3, False)
    arrive(3)
    slide(y_inverse(3), True)


def on_device(slip_rate, slip_field, prestress, history, kernel, band_len, mode_band):
    vmem = pl.BlockSpec(memory_space=pltpu.VMEM)
    smem = pl.BlockSpec(memory_space=pltpu.SMEM)
    constants = [jnp.asarray(table) for table in tables()]
    shape = jax.ShapeDtypeStruct((3, 8, N), F32)
    dma = pltpu.SemaphoreType.DMA
    return pl.pallas_call(
        body,
        out_shape=(shape, shape),
        in_specs=[vmem] * (5 + len(constants)) + [smem] * 2,
        out_specs=(vmem, vmem),
        scratch_shapes=[
            pltpu.VMEM((4, DEV, 2, 128), F32),
            pltpu.VMEM((4, DEV, 2, 128), F32),
            pltpu.VMEM((384, 256), F32),
            pltpu.VMEM((128, 256), F32),
            pltpu.VMEM((2, 256, 128), F32),
            pltpu.VMEM((2, 256, 128), F32),
            pltpu.VMEM((8, N), jnp.int32),
            dma((4,)), dma((4,)), dma((2,)), dma((2,)), dma((1,)),
        ],
        compiler_params=pltpu.CompilerParams(
            collective_id=0, has_side_effects=True, vmem_limit_bytes=56 * 1024 * 1024
        ),
    )(slip_rate, slip_field, prestress, history, mode_band, *constants, kernel.reshape(-1), band_len)


def solution(mesh):
    rows = P(None, ("kx", "ky"), None)
    return jax.shard_map(
        on_device,
        mesh=mesh,
        in_specs=(
            rows, rows, rows, P(None, None, None, ("kx", "ky"), None), P(), P(), P(("kx", "ky"), None),
        ),
        out_specs=(rows, rows),
        check_vma=False,
    )
```

profile of v0, /device:TPU:1, one launch (start us, length us, event | category | flops | bytes accessed | tf_op | source)
XLA Modules:
  0.0 90.5 jit_solution(295313719228067814)
XLA Ops:
  0.6 0.8 copy.18
  1.5 0.7 reshape.7.kern
  2.2 85.1 %shard_map.167 = (f32[3,8,2048]{2,1,0:T(8,128)}, f32[3,8,2048]{2,1,0:T(8,128)}) custom-call(f32[3,8,2048]{2,1,0:T(8,128)} %slip_rate.1, f32[3,8,2048]{2,1,0:T(8,128)} %slip_field.1, f32[3,8,2048]{2,1,0:T(8,128)} %prestress.1, bf16[6,3,2,8,2048]{4,3,2,1,0:T(8,128)(2,1)} %history.1, s32[8,2048]{1,0:T(8,128)} %mode_band.1, ...), custom_call_target="tpu_custom_call" | custom-call | tf_op jit(solution)/shard_map/pallas_call | solution.py:420
  87.3 1.6 %copy.21 = f32[3,8,2048]{2,1,0:T(8,128)} copy(f32[3,8,2048]{2,1,0:T(8,128)} %get-tuple-element.4) | data formatting | bytes 393216
  88.9 1.6 %copy.22 = f32[3,8,2048]{2,1,0:T(8,128)} copy(f32[3,8,2048]{2,1,0:T(8,128)} %get-tuple-element.5) | data formatting | bytes 393216
where the time goes:
time: 90.7 us; the launch traced here: 90.5 us
  Pallas kernels  85.1 us (94%)
  local copies, waits for them, and re-layouts  4.76 us (5%)
    pallas_call x1, Pallas kernels, on_device(): pl.pallas_call(body, out_shape=(shape, shape), in_specs=[vmem] * (5 + len...  85.1 us
    unnamed x3, local copies, waits for them, and re-layouts  4.05 us

commit v1 on v0

--- a/solution.py
+++ b/solution.py
@@ -43,12 +43,10 @@
     y_twist = np.stack([np.cos(angle), np.sin(angle)]).astype(np.float32)
     x_twist = np.zeros((2, 256, 128), np.float32)
     eight = np.arange(8)
-    for slot in range(SLOTS):
-        for comp in range(3):
-            at = lane(slot, comp, 0)
-            angle = 2 * np.pi / N * (np.arange(256)[:, None] * eight[None, :])
-            x_twist[0, :, at : at + 8] = np.cos(angle)
-            x_twist[1, :, at : at + 8] = np.sin(angle)
+    for group in range(16):
+        angle = 2 * np.pi / N * (np.arange(256)[:, None] * eight[None, :])
+        x_twist[0, :, group * 8 : group * 8 + 8] = np.cos(angle)
+        x_twist[1, :, group * 8 : group * 8 + 8] = np.sin(angle)
     angle = 2 * np.pi / 8 * (eight[:, None] * eight[None, :] % 8)
     cos8, sin8 = np.cos(angle), np.sin(angle)
     forward = np.zeros((256, 256))
@@ -62,22 +60,34 @@
             inverse[re, re], inverse[im, re] = cos8, -sin8
             inverse[re, im], inverse[im, im] = sin8, cos8
     eights = np.stack([split(forward), split(inverse)])
-    own_rows = [{0: 0, 1: 1, 2: 2, 3: 3}, {0: 4, 1: 3, 2: 2, 3: 1, 4: 0}]
-    sent_rows = [{0: 4, 1: 5, 2: 6, 3: 7}, {1: 7, 2: 6, 3: 5}]
     past = np.zeros((2, 384, 512))
-    for half in range(2):
-        for block, rows in enumerate((own_rows[half], sent_rows[half])):
-            for slot, row in rows.items():
-                for comp in range(3):
-                    out = block * 256 + lane(slot, comp, 0)
-                    re, im = slice(out, out + 8), slice(out + 128, out + 136)
-                    for mode in range(8):
-                        in_re = ((comp * 2 + 0) * 8 + mode) * 8 + row
-                        in_im = ((comp * 2 + 1) * 8 + mode) * 8 + row
-                        past[half, in_re, re] = cos8[mode]
-                        past[half, in_im, re] = -sin8[mode]
-                        past[half, in_re, im] = sin8[mode]
-                        past[half, in_im, im] = cos8[mode]
+
+    def fill(table, out_re, out_im, comp, row, turned):
+        re, im = slice(out_re, out_re + 8), slice(out_im, out_im + 8)
+        for mode in range(8):
+            in_re = ((comp * 2 + 0) * 8 + mode) * 8 + row
+            in_im = ((comp * 2 + 1) * 8 + mode) * 8 + row
+            if turned:
+                table[in_re, re], table[in_im, re] = sin8[mode], cos8[mode]
+                table[in_re, im], table[in_im, im] = -cos8[mode], sin8[mode]
+            else:
+                table[in_re, re], table[in_im, re] = cos8[mode], -sin8[mode]
+                table[in_re, im], table[in_im, im] = sin8[mode], cos8[mode]
+
+    for half, (own, other) in enumerate((((0, 1, 2, 3, 4), (5, 6, 7)), ((4, 3, 2, 1, 0), (7, 6, 5)))):
+        for slot, row in enumerate(own):
+            for comp in range(3):
+                at = lane(slot, comp, 0)
+                fill(past[half], at, 128 + at, comp, row, False)
+        for slot, row in enumerate(other):
+            for comp in range(3):
+                group = slot * 3 + comp
+                if group == 8:
+                    fill(past[half], 120, 248, comp, row, False)
+                else:
+                    at = 256 + group * 8
+                    fill(past[half], at, 128 + at, comp, row, False)
+                    fill(past[half], at + 64, 192 + at, comp, row, True)
     past = np.stack([split(past[0]), split(past[1])])
     picks = np.zeros((2, 3, 128, 128), np.float32)
     missing = np.full((2, 2, 8, 128), 8.0, np.float32)
@@ -124,13 +134,28 @@
     return 2 * device + (device // 128) * (511 - 4 * device)
 
 
+def slide(stress, coeff):
+    strength = coeff * softplus(-stress[2])
+    magnitude = jnp.sqrt(stress[0] * stress[0] + stress[1] * stress[1] + 1.0)
+    ratio = softplus(magnitude - strength) / magnitude
+    return ratio * stress[0], ratio * stress[1], softplus(stress[2])
+
+
+def weakening(first, second):
+    worn = jnp.sqrt(first * first + second * second + 1.0) - 1.0
+    return 0.35 + 0.35 * jnp.exp(worn * -2.0)
+
+
 def body(
+    slip_rate_in, slip_field_in, prestress_in, history_in, mode_band_in,
+    y_table_in, x_table_in, y_twist_in, x_twist_in, eights_in, past_in, picks_in, missing_in, turn_in,
+    kern, band_len,
+    stress_out,
     slip_rate, slip_field, prestress, history, mode_band,
     y_table, x_table, y_twist, x_twist, eights, past, picks, missing, turn,
-    kern, band_len,
-    new_rate, new_slip,
-    send, recv, stacked, bands, given, taken, partner_band,
-    send_sem, recv_sem, pair_send, pair_recv, own_sem,
+    send_0, send_1, send_2, send_3, recv_0, recv_1, recv_2, recv_3,
+    stacked, bands, hold, kept, partner_band,
+    send_sem, recv_sem, pair_send, pair_recv, load_sem,
 ):
     kx, ky = lax.axis_index("kx"), lax.axis_index("ky")
     me = kx * 8 + ky
@@ -138,6 +163,28 @@
     mine = block_of(me)
     partner = 255 - me
     partner_id = (partner // 8, lax.rem(partner, 8))
+    send, recv = (send_0, send_1, send_2, send_3), (recv_0, recv_1, recv_2, recv_3)
+
+    partner_band[0:4] = jnp.zeros((4, N), jnp.int32)
+    loads = {}
+    for at, (name, source, target) in enumerate((
+        ("slip_rate", slip_rate_in, slip_rate),
+        ("y_twist", y_twist_in, y_twist),
+        ("y_table", y_table_in, y_table),
+        ("mode_band", mode_band_in, mode_band),
+        ("history", history_in, history),
+        ("past", past_in.at[half], past),
+        ("x_twist", x_twist_in, x_twist),
+        ("x_table", x_table_in, x_table),
+        ("turn", turn_in, turn),
+        ("picks", picks_in.at[half], picks),
+        ("missing", missing_in.at[half], missing),
+        ("eights", eights_in, eights),
+        ("slip_field", slip_field_in, slip_field),
+        ("prestress", prestress_in, prestress),
+    )):
+        loads[name] = pltpu.make_async_copy(source, target, load_sem.at[at])
+        loads[name].start()
 
     barrier = pltpu.get_barrier_semaphore()
 
@@ -148,42 +195,46 @@
         )
         return carry
 
-    lax.fori_loop(1, DEV, greet, 0)
+    lax.fori_loop(1, DEV, greet, 0, unroll=5)
 
     def exchange(turn_at, forward):
         def one(device):
             if forward:
-                source, target = send.at[turn_at, block_of(device)], recv.at[turn_at, me]
+                source, target = send[turn_at].at[block_of(device)], recv[turn_at].at[me]
             else:
-                source, target = send.at[turn_at, device], recv.at[turn_at, mine]
+                source, target = send[turn_at].at[device], recv[turn_at].at[mine]
             pltpu.make_async_remote_copy(
                 source, target, send_sem.at[turn_at], recv_sem.at[turn_at],
                 device_id=(device // 8, lax.rem(device, 8)), device_id_type=MESH,
             ).start()
 
         one(lax.rem(me + 128, DEV))
+        one(lax.rem(me + 129, DEV))
+        one(lax.rem(me + 127, DEV))
 
         def two(step, carry):
             one(lax.rem(me + 128 + step, DEV))
             one(lax.rem(me + 128 - step, DEV))
             return carry
 
-        lax.fori_loop(1, 128, two, 0)
+        lax.fori_loop(2, 128, two, 0, unroll=7)
         if forward:
-            source, target = send.at[turn_at, mine], recv.at[turn_at, me]
+            source, target = send[turn_at].at[mine], recv[turn_at].at[me]
         else:
-            source, target = send.at[turn_at, me], recv.at[turn_at, mine]
+            source, target = send[turn_at].at[me], recv[turn_at].at[mine]
         pltpu.make_async_copy(source, target, recv_sem.at[turn_at]).start()
 
     def arrive(turn_at):
-        whole = recv.at[turn_at]
+        whole = recv[turn_at]
         pltpu.make_async_copy(whole, whole, recv_sem.at[turn_at]).wait()
-        gone = send.at[turn_at, pl.ds(0, DEV - 1)]
+
+    def sent(turn_at):
+        gone = send[turn_at].at[pl.ds(0, DEV - 1)]
         pltpu.make_async_copy(gone, gone, send_sem.at[turn_at]).wait()
 
-    def put(turn_at, re, im):
-        send[turn_at, :, 0, :] = re
-        send[turn_at, :, 1, :] = im
+    def put(turn_at, *rows):
+        for at, row in enumerate(rows):
+            send[turn_at][:, at, :] = row
 
     def y_forward(field):
         cos, sin = y_twist[0], y_twist[1]
@@ -218,9 +269,19 @@
         )
         return out[:, :128], out[:, 128:]
 
+    def swap(value):
+        even = lax.rem(lax.broadcasted_iota(jnp.int32, value.shape, 1), 2) == 0
+        return jnp.where(even, pltpu.roll(value, 255, 1), pltpu.roll(value, 1, 1))
+
     def y_inverse(turn_at):
-        re = halves(recv[turn_at, :, 0, :].T)
-        im = halves(recv[turn_at, :, 1, :].T)
+        re = recv[turn_at][:, 0, :].T
+        im = recv[turn_at][:, 1, :].T
+        if turn_at == 1:
+            rest = recv[turn_at][:, 2, :].T
+            kept[0] = swap(jnp.concatenate([rest[0:64], re[120:128]], 0))
+            kept[1] = swap(jnp.concatenate([rest[64:128], im[120:128]], 0))
+        re = halves(jnp.concatenate([re[:24], re[24:96] + kept[0], re[96:]], 0))
+        im = halves(jnp.concatenate([im[:24], im[24:96] + kept[1], im[96:]], 0))
 
         def arrange(r, i):
             return jnp.concatenate([jnp.concatenate([r, -i], 1), jnp.concatenate([i, r], 1)], 0)
@@ -271,7 +332,7 @@
         return re * cos - im * sin, im * cos + re * sin
 
     def x_forward(turn_at):
-        re, im = x_transform(recv[turn_at, :, 0, :], recv[turn_at, :, 1, :], -1)
+        re, im = x_transform(recv[turn_at][:, 0, :], recv[turn_at][:, 1, :], -1)
         re, im = twist(re, im, -1)
         out = product(halves(jnp.concatenate([re, im], 1)), (eights[0, 0], eights[0, 1]))
         return out[:, :128], out[:, 128:]
@@ -281,24 +342,22 @@
         re, im = twist(out[:, :128], out[:, 128:], 1)
         return x_transform(re, im, 1)
 
+    for name in ("slip_rate", "y_twist", "y_table"):
+        loads[name].wait()
     put(0, *y_forward([slip_rate[comp] for comp in range(3)]))
-    pl.semaphore_wait(barrier, DEV - 1)
-    exchange(0, True)
-    band_copy = pltpu.make_async_remote_copy(
-        mode_band, partner_band, pair_send.at[0], pair_recv.at[0],
-        device_id=partner_id, device_id_type=MESH,
-    )
-    band_copy.start()
 
     def live(band, lag, comp):
         kept = (band_len[band] > lag).astype(F32)
-        return kern[(band * LAGS + lag) * 3 + comp] * kept
+        return kern[comp, band, lag] * kept
 
     effective = {
         (band, lag, comp): live(band, lag, comp)
         for lag in (0, 1, 2, 3) for comp in range(3) for band in range(BANDS)
     }
     effective.update({(0, lag, comp): live(0, lag, comp) for lag in range(4, LAGS) for comp in range(3)})
+
+    for name in ("mode_band", "history", "past", "x_twist", "x_table"):
+        loads[name].wait()
 
     def gather(mode, carry):
         at = pl.multiple_of(mode * 256, 256)
@@ -322,16 +381,29 @@
 
     lax.fori_loop(0, 8, gather, 0)
     flat = halves(stacked[...].T)
-    out = product(flat, (past[half, 0], past[half, 1]))
-    given_re, given_im = x_transform(*twist(out[:, 256:384], out[:, 384:], 1), 1)
-    given[0] = given_re
-    given[1] = given_im
-    given_copy = pltpu.make_async_remote_copy(
-        given, taken, pair_send.at[1], pair_recv.at[1],
+    out = product(flat, (past[0], past[1]))
+    sign = 1.0 - 2.0 * half.astype(F32)
+    held_re, held_im = x_transform(*twist(out[:, :128], out[:, 128:256], 1), 1)
+    hold[0] = held_re
+    hold[1] = held_im * sign
+    rest_re, rest_im = twist(out[:, 256:384], out[:, 384:], 1)
+    rest_re, rest_im = halves(rest_re), halves(rest_im)
+    rest = product(
+        (x_table[0], x_table[1]),
+        tuple(jnp.concatenate([rest_re[n], -rest_im[n]], 0) for n in range(2)),
+    )
+    lane_at = lax.broadcasted_iota(jnp.int32, (1, 128), 1)
+    send_1[:, 2, :] = rest * jnp.where(lane_at < 64, 1.0, sign)
+
+    pl.semaphore_wait(barrier, DEV - 1)
+    band_copy = pltpu.make_async_remote_copy(
+        mode_band.at[pl.ds(4, 4)], partner_band.at[pl.ds(4, 4)], pair_send.at[0], pair_recv.at[0],
         device_id=partner_id, device_id_type=MESH,
     )
-    given_copy.start()
-    own_re, own_im = x_transform(*twist(out[:, :128], out[:, 128:256], 1), 1)
+    band_copy.start()
+    exchange(0, True)
+    for name in ("turn", "picks", "missing", "eights", "slip_field", "prestress"):
+        loads[name].wait()
 
     band_copy.wait()
     for mode in range(8):
@@ -340,12 +412,11 @@
     dot = functools.partial(lax.dot_general, dimension_numbers=NN, preferred_element_type=F32)
     turned = dot(turn[...], plain).astype(BF16)
     first_row = lax.broadcasted_iota(jnp.int32, (256, 128), 0) == 0
-    plain_band = dot(plain, picks[half, 0]) + missing[half, 0, 0:1]
+    plain_band = dot(plain, picks[0]) + missing[0, 0:1]
     turned_band = (
-        jnp.where(first_row, dot(turned, picks[half, 2]), dot(turned, picks[half, 1]))
-        + missing[half, 1, 0:1]
+        jnp.where(first_row, dot(turned, picks[2]), dot(turned, picks[1]))
+        + missing[1, 0:1]
     )
-    lane_at = lax.broadcasted_iota(jnp.int32, (1, 128), 1)
     lane_comp = lax.rem(lane_at // 8, 3)
     weight = [jnp.zeros((256, 128), F32) for _ in range(2)]
     for which in (plain_band, turned_band):
@@ -363,79 +434,80 @@
     now_weight = weight[1] + 0.5 * weight[0]
     tried_weight = 0.5 * weight[0]
 
-    given_copy.wait()
-    sign = 1.0 - 2.0 * half.astype(F32)
-    held_re = own_re + taken[0]
-    held_im = sign * (own_im - taken[1])
-
-    slip = [slip_field[comp] for comp in range(2)]
-    worn = jnp.sqrt(slip[0] * slip[0] + slip[1] * slip[1] + 1.0) - 1.0
-    coeff = 0.35 + 0.35 * jnp.exp(worn * -2.0)
-
-    def slide(field, write):
-        rates = [[], [], []]
-        for n in range(4):
-            part = slice(512 * n, 512 * (n + 1))
-            s = [prestress[comp, :, part] + field[comp][n] for comp in range(3)]
-            strength = coeff[:, part] * softplus(-s[2])
-            magnitude = jnp.sqrt(s[0] * s[0] + s[1] * s[1] + 1.0)
-            ratio = softplus(magnitude - strength) / magnitude
-            for comp, value in enumerate((ratio * s[0], ratio * s[1], softplus(s[2]))):
-                if write:
-                    new_rate[comp, :, part] = value
-                    new_slip[comp, :, part] = slip_field[comp, :, part] + 0.25 * (
-                        slip_rate[comp, :, part] + value
-                    )
-                rates[comp].append(value)
-        return [jnp.concatenate(rate, 1) for rate in rates]
+    coeff = weakening(slip_field[0], slip_field[1])
 
     arrive(0)
     now_re, now_im = x_forward(0)
     re, im = x_inverse(now_re * first_weight, now_im * first_weight)
-    put(1, re + held_re, im + held_im)
+    put(1, re + hold[0], im + hold[1])
     exchange(1, False)
     re, im = x_inverse(now_re * now_weight, now_im * now_weight)
-    given[0] = re + held_re
-    given[1] = im + held_im
+    hold[0] = re + hold[0]
+    hold[1] = im + hold[1]
     arrive(1)
-    first = slide(y_inverse(1), False)
-
-    put(2, *y_forward(first))
+    field = y_inverse(1)
+    stress = [prestress[comp] + jnp.concatenate(field[comp], 1) for comp in range(3)]
+
+    put(2, *y_forward(slide(stress, coeff)))
     exchange(2, True)
     arrive(2)
     re, im = x_forward(2)
     re, im = x_inverse(re * tried_weight, im * tried_weight)
-    put(3, re + given[0], im + given[1])
+    put(3, re + hold[0], im + hold[1])
     exchange(3, False)
     arrive(3)
-    slide(y_inverse(3), True)
+    field = y_inverse(3)
+    for comp in range(3):
+        for n in range(4):
+            part = slice(512 * n, 512 * (n + 1))
+            stress_out[comp, :, part] = prestress[comp, :, part] + field[comp][n]
+    for turn_at in range(4):
+        sent(turn_at)
+
+
+def finish(stress, slip_field, slip_rate, new_rate, new_slip):
+    coeff = weakening(slip_field[0], slip_field[1])
+    for comp, value in enumerate(slide([stress[comp] for comp in range(3)], coeff)):
+        new_rate[comp] = value
+        new_slip[comp] = slip_field[comp] + 0.25 * (slip_rate[comp] + value)
 
 
 def on_device(slip_rate, slip_field, prestress, history, kernel, band_len, mode_band):
     vmem = pl.BlockSpec(memory_space=pltpu.VMEM)
     smem = pl.BlockSpec(memory_space=pltpu.SMEM)
+    anywhere = pl.BlockSpec(memory_space=pltpu.HBM)
     constants = [jnp.asarray(table) for table in tables()]
+    halved = (5, 6, 7)
     shape = jax.ShapeDtypeStruct((3, 8, N), F32)
     dma = pltpu.SemaphoreType.DMA
-    return pl.pallas_call(
+    inputs = (slip_rate, slip_field, prestress, history, mode_band)
+    stress = pl.pallas_call(
         body,
-        out_shape=(shape, shape),
-        in_specs=[vmem] * (5 + len(constants)) + [smem] * 2,
-        out_specs=(vmem, vmem),
+        out_shape=shape,
+        in_specs=[anywhere] * (5 + len(constants)) + [smem] * 2,
+        out_specs=vmem,
         scratch_shapes=[
-            pltpu.VMEM((4, DEV, 2, 128), F32),
-            pltpu.VMEM((4, DEV, 2, 128), F32),
+            *[pltpu.VMEM(value.shape, value.dtype) for value in inputs],
+            *[
+                pltpu.VMEM(value.shape[1:] if at in halved else value.shape, value.dtype)
+                for at, value in enumerate(constants)
+            ],
+            *[pltpu.VMEM((DEV, 3 if at == 1 else 2, 128), F32) for at in (0, 1, 2, 3)] ,
+            *[pltpu.VMEM((DEV, 3 if at == 1 else 2, 128), F32) for at in (0, 1, 2, 3)],
             pltpu.VMEM((384, 256), F32),
             pltpu.VMEM((128, 256), F32),
             pltpu.VMEM((2, 256, 128), F32),
-            pltpu.VMEM((2, 256, 128), F32),
+            pltpu.VMEM((2, 72, 256), F32),
             pltpu.VMEM((8, N), jnp.int32),
-            dma((4,)), dma((4,)), dma((2,)), dma((2,)), dma((1,)),
+            dma((4,)), dma((4,)), dma((1,)), dma((1,)), dma((14,)),
         ],
         compiler_params=pltpu.CompilerParams(
-            collective_id=0, has_side_effects=True, vmem_limit_bytes=56 * 1024 * 1024
+            collective_id=0, has_side_effects=True, vmem_limit_bytes=67043328
         ),
-    )(slip_rate, slip_field, prestress, history, mode_band, *constants, kernel.reshape(-1), band_len)
+    )(*inputs, *constants, jnp.transpose(kernel, (2, 0, 1)), band_len)
+    return pl.pallas_call(
+        finish, out_shape=(shape, shape), in_specs=[vmem] * 3, out_specs=(vmem, vmem)
+    )(stress, slip_field, slip_rate)
 
 
 def solution(mesh):

time: 90.7 us -> 75.5 us (0.83)
  Pallas kernels: 85.1 us -> 74.7 us
  local copies, waits for them, and re-layouts: 4.76 us -> 0 us
    pallas_call x1 -> x2, Pallas kernels: 85.1 us -> 74.7 us  [the longest x1 72.7 us: on_device(): pl.pallas_call(body, out_shape=shape, in_specs=[anywhere] * (5 + len(cons...]
    unnamed x3 -> x0, local copies, waits for them, and re-layouts: 4.05 us -> none
where the time goes in v1:
time: 75.5 us; the launch traced here: 75.3 us
  Pallas kernels  74.7 us (99%)
    pallas_call x1, Pallas kernels, on_device(): pl.pallas_call(body, out_shape=shape, in_specs=[anywhere] * (5 + len(cons...  72.7 us
    pallas_call x1, Pallas kernels, on_device(): pl.pallas_call(finish, out_shape=(shape, shape), in_specs=[vmem] * 3, out...  2.06 us

profile of v1, /device:TPU:1, one launch (start us, length us, event | category | flops | bytes accessed | tf_op | source)
XLA Modules:
  0.0 75.3 jit_solution(13899168072987576582)
XLA Ops:
  0.6 72.7 %shard_map.167.stress = f32[3,8,2048]{2,1,0:T(8,128)} custom-call(f32[3,8,2048]{2,1,0:T(8,128)} %slip_rate.1, f32[3,8,2048]{2,1,0:T(8,128)} %slip_field.1, f32[3,8,2048]{2,1,0:T(8,128)} %prestress_in.1, bf16[6,3,2,8,2048]{4,3,2,1,0:T(8,128)(2,1)} %history_in.1, s32[8,2048]{1,0:T(8,128)} %mode_band_in.1, bf16[2,256,1024]{2,1,0:T(8,128)(2,1)} %constant.18.clone.y_table_in, ...), custom_call_target="tpu_custom_call" | custom-call | tf_op jit(solution)/shard_map/pallas_call | solution.py:484
  73.3 2.1 %shard_map.168 = (f32[3,8,2048]{2,1,0:T(8,128)}, f32[3,8,2048]{2,1,0:T(8,128)}) custom-call(f32[3,8,2048]{2,1,0:T(8,128)} %shard_map.167.stress, f32[3,8,2048]{2,1,0:T(8,128)} %slip_field.1, f32[3,8,2048]{2,1,0:T(8,128)} %slip_rate.1), custom_call_target="tpu_custom_call" | custom-call | tf_op jit(solution)/shard_map/pallas_call | solution.py:508

commit v2 on v1

--- a/solution.py
+++ b/solution.py
@@ -153,7 +153,7 @@
     stress_out,
     slip_rate, slip_field, prestress, history, mode_band,
     y_table, x_table, y_twist, x_twist, eights, past, picks, missing, turn,
-    send_0, send_1, send_2, send_3, recv_0, recv_1, recv_2, recv_3,
+    send_0, send_1, send_2, send_3, send_4, recv_0, recv_1, recv_2, recv_3, recv_4,
     stacked, bands, hold, kept, partner_band,
     send_sem, recv_sem, pair_send, pair_recv, load_sem,
 ):
@@ -163,7 +163,8 @@
     mine = block_of(me)
     partner = 255 - me
     partner_id = (partner // 8, lax.rem(partner, 8))
-    send, recv = (send_0, send_1, send_2, send_3), (recv_0, recv_1, recv_2, recv_3)
+    send = (send_0, send_1, send_2, send_3, send_4)
+    recv = (recv_0, recv_1, recv_2, recv_3, recv_4)
 
     partner_band[0:4] = jnp.zeros((4, N), jnp.int32)
     loads = {}
@@ -188,14 +189,20 @@
 
     barrier = pltpu.get_barrier_semaphore()
 
-    def greet(step, carry):
-        other = lax.rem(me + step, DEV)
+    def greet(other):
         pl.semaphore_signal(
             barrier, inc=1, device_id=(other // 8, lax.rem(other, 8)), device_id_type=MESH
         )
+
+    def greet_two(step, carry):
+        greet(lax.rem(me + 128 + step, DEV))
+        greet(lax.rem(me + 128 - step, DEV))
         return carry
 
-    lax.fori_loop(1, DEV, greet, 0, unroll=5)
+    greet(lax.rem(me + 128, DEV))
+    greet(lax.rem(me + 129, DEV))
+    greet(lax.rem(me + 127, DEV))
+    lax.fori_loop(2, 128, greet_two, 0, unroll=7)
 
     def exchange(turn_at, forward):
         def one(device):
@@ -277,7 +284,8 @@
         re = recv[turn_at][:, 0, :].T
         im = recv[turn_at][:, 1, :].T
         if turn_at == 1:
-            rest = recv[turn_at][:, 2, :].T
+            arrive(4)
+            rest = recv[4][:, 0, :].T
             kept[0] = swap(jnp.concatenate([rest[0:64], re[120:128]], 0))
             kept[1] = swap(jnp.concatenate([rest[64:128], im[120:128]], 0))
         re = halves(jnp.concatenate([re[:24], re[24:96] + kept[0], re[96:]], 0))
@@ -393,7 +401,7 @@
         tuple(jnp.concatenate([rest_re[n], -rest_im[n]], 0) for n in range(2)),
     )
     lane_at = lax.broadcasted_iota(jnp.int32, (1, 128), 1)
-    send_1[:, 2, :] = rest * jnp.where(lane_at < 64, 1.0, sign)
+    send_4[:, 0, :] = rest * jnp.where(lane_at < 64, 1.0, sign)
 
     pl.semaphore_wait(barrier, DEV - 1)
     band_copy = pltpu.make_async_remote_copy(
@@ -402,6 +410,7 @@
     )
     band_copy.start()
     exchange(0, True)
+    exchange(4, False)
     for name in ("turn", "picks", "missing", "eights", "slip_field", "prestress"):
         loads[name].wait()
 
@@ -461,7 +470,7 @@
         for n in range(4):
             part = slice(512 * n, 512 * (n + 1))
             stress_out[comp, :, part] = prestress[comp, :, part] + field[comp][n]
-    for turn_at in range(4):
+    for turn_at in range(5):
         sent(turn_at)
 
 
@@ -492,14 +501,13 @@
                 pltpu.VMEM(value.shape[1:] if at in halved else value.shape, value.dtype)
                 for at, value in enumerate(constants)
             ],
-            *[pltpu.VMEM((DEV, 3 if at == 1 else 2, 128), F32) for at in (0, 1, 2, 3)] ,
-            *[pltpu.VMEM((DEV, 3 if at == 1 else 2, 128), F32) for at in (0, 1, 2, 3)],
+            *[pltpu.VMEM((DEV, rows, 128), F32) for rows in (2, 2, 2, 2, 1) * 2],
             pltpu.VMEM((384, 256), F32),
             pltpu.VMEM((128, 256), F32),
             pltpu.VMEM((2, 256, 128), F32),
             pltpu.VMEM((2, 72, 256), F32),
             pltpu.VMEM((8, N), jnp.int32),
-            dma((4,)), dma((4,)), dma((1,)), dma((1,)), dma((14,)),
+            dma((5,)), dma((5,)), dma((1,)), dma((1,)), dma((14,)),
         ],
         compiler_params=pltpu.CompilerParams(
             collective_id=0, has_side_effects=True, vmem_limit_bytes=67043328

time: 75.5 us -> 73.5 us (0.974)
  Pallas kernels: 74.7 us -> 72.7 us
    pallas_call x1, Pallas kernels: 72.7 us -> 70.6 us  [on_device(): pl.pallas_call(body, out_shape=shape, in_specs=[anywhere] * (5 + len(cons...]
where the time goes in v2:
time: 73.5 us; the launch traced here: 73.3 us
  Pallas kernels  72.7 us (99%)
    pallas_call x1, Pallas kernels, on_device(): pl.pallas_call(body, out_shape=shape, in_specs=[anywhere] * (5 + len(cons...  70.6 us
    pallas_call x1, Pallas kernels, on_device(): pl.pallas_call(finish, out_shape=(shape, shape), in_specs=[vmem] * 3, out...  2.06 us

profile of v2, /device:TPU:1, one launch (start us, length us, event | category | flops | bytes accessed | tf_op | source)
XLA Modules:
  0.0 73.3 jit_solution(4503170078326879373)
XLA Ops:
  0.6 70.6 %shard_map.167.stress = f32[3,8,2048]{2,1,0:T(8,128)} custom-call(f32[3,8,2048]{2,1,0:T(8,128)} %slip_rate.1, f32[3,8,2048]{2,1,0:T(8,128)} %slip_field.1, f32[3,8,2048]{2,1,0:T(8,128)} %prestress_in.1, bf16[6,3,2,8,2048]{4,3,2,1,0:T(8,128)(2,1)} %history_in.1, s32[8,2048]{1,0:T(8,128)} %mode_band_in.1, bf16[2,256,1024]{2,1,0:T(8,128)(2,1)} %constant.18.clone.y_table_in, ...), custom_call_target="tpu_custom_call" | custom-call | tf_op jit(solution)/shard_map/pallas_call | solution.py:493
  71.3 2.1 %shard_map.168 = (f32[3,8,2048]{2,1,0:T(8,128)}, f32[3,8,2048]{2,1,0:T(8,128)}) custom-call(f32[3,8,2048]{2,1,0:T(8,128)} %shard_map.167.stress, f32[3,8,2048]{2,1,0:T(8,128)} %slip_field.1, f32[3,8,2048]{2,1,0:T(8,128)} %slip_rate.1), custom_call_target="tpu_custom_call" | custom-call | tf_op jit(solution)/shard_map/pallas_call | solution.py:516

commit v3 on v2

--- a/solution.py
+++ b/solution.py
@@ -131,7 +131,7 @@
 
 
 def block_of(device):
-    return 2 * device + (device // 128) * (511 - 4 * device)
+    return 2 * device + lax.div(device, 128) * (511 - 4 * device)
 
 
 def slide(stress, coeff):
@@ -165,6 +165,23 @@
     partner_id = (partner // 8, lax.rem(partner, 8))
     send = (send_0, send_1, send_2, send_3, send_4)
     recv = (recv_0, recv_1, recv_2, recv_3, recv_4)
+
+    barrier = pltpu.get_barrier_semaphore()
+
+    def greet(other):
+        pl.semaphore_signal(
+            barrier, inc=1, device_id=(lax.div(other, 8), lax.rem(other, 8)), device_id_type=MESH
+        )
+
+    def greet_two(step, carry):
+        greet(lax.rem(me + 128 + step, DEV))
+        greet(lax.rem(me + 128 - step, DEV))
+        return carry
+
+    greet(lax.rem(me + 128, DEV))
+    greet(lax.rem(me + 129, DEV))
+    greet(lax.rem(me + 127, DEV))
+    lax.fori_loop(2, 128, greet_two, 0, unroll=7)
 
     partner_band[0:4] = jnp.zeros((4, N), jnp.int32)
     loads = {}
@@ -187,23 +204,6 @@
         loads[name] = pltpu.make_async_copy(source, target, load_sem.at[at])
         loads[name].start()
 
-    barrier = pltpu.get_barrier_semaphore()
-
-    def greet(other):
-        pl.semaphore_signal(
-            barrier, inc=1, device_id=(other // 8, lax.rem(other, 8)), device_id_type=MESH
-        )
-
-    def greet_two(step, carry):
-        greet(lax.rem(me + 128 + step, DEV))
-        greet(lax.rem(me + 128 - step, DEV))
-        return carry
-
-    greet(lax.rem(me + 128, DEV))
-    greet(lax.rem(me + 129, DEV))
-    greet(lax.rem(me + 127, DEV))
-    lax.fori_loop(2, 128, greet_two, 0, unroll=7)
-
     def exchange(turn_at, forward):
         def one(device):
             if forward:
@@ -212,7 +212,7 @@
                 source, target = send[turn_at].at[device], recv[turn_at].at[mine]
             pltpu.make_async_remote_copy(
                 source, target, send_sem.at[turn_at], recv_sem.at[turn_at],
-                device_id=(device // 8, lax.rem(device, 8)), device_id_type=MESH,
+                device_id=(lax.div(device, 8), lax.rem(device, 8)), device_id_type=MESH,
             ).start()
 
         one(lax.rem(me + 128, DEV))
@@ -510,11 +510,12 @@
             dma((5,)), dma((5,)), dma((1,)), dma((1,)), dma((14,)),
         ],
         compiler_params=pltpu.CompilerParams(
-            collective_id=0, has_side_effects=True, vmem_limit_bytes=67043328
+            collective_id=0, has_side_effects=True, vmem_limit_bytes=62 * 1024 * 1024
         ),
     )(*inputs, *constants, jnp.transpose(kernel, (2, 0, 1)), band_len)
     return pl.pallas_call(
-        finish, out_shape=(shape, shape), in_specs=[vmem] * 3, out_specs=(vmem, vmem)
+        finish, out_shape=(shape, shape), in_specs=[vmem] * 3, out_specs=(vmem, vmem),
+        compiler_params=pltpu.CompilerParams(vmem_limit_bytes=4 * 1024 * 1024),
     )(stress, slip_field, slip_rate)
 
 

time: 73.5 us -> 72.2 us (0.982)
  Pallas kernels: 72.7 us -> 70.4 us
  local copies, waits for them, and re-layouts: 0 us -> 0.93 us
    pallas_call x1, Pallas kernels: 70.6 us -> 69.5 us  [on_device(): pl.pallas_call(body, out_shape=shape, in_specs=[anywhere] * (5 + len(cons...]
    pallas_call x1, Pallas kernels: 2.06 us -> 0.94 us  [on_device(): pl.pallas_call(finish, out_shape=(shape, shape), in_specs=[vmem] * 3, out...]
    unnamed x0 -> x6, local copies, waits for them, and re-layouts: none -> 0.93 us
where the time goes in v3:
time: 72.2 us; the launch traced here: 72 us
  Pallas kernels  70.4 us (98%)
  local copies, waits for them, and re-layouts  0.93 us (1%)
    pallas_call x1, Pallas kernels, on_device(): pl.pallas_call(body, out_shape=shape, in_specs=[anywhere] * (5 + len(cons...  69.5 us

profile of v3, /device:TPU:1, one launch (start us, length us, event | category | flops | bytes accessed | tf_op | source)
XLA Modules:
  0.0 72.0 jit_solution(15267536787306840483)
XLA Ops:
  0.6 0.0 copy-start
  0.6 0.0 copy-start.1
  0.7 69.5 %shard_map.167.stress = f32[3,8,2048]{2,1,0:T(8,128)} custom-call(f32[3,8,2048]{2,1,0:T(8,128)} %slip_rate.1, f32[3,8,2048]{2,1,0:T(8,128)} %slip_field.1, f32[3,8,2048]{2,1,0:T(8,128)} %prestress_in.1, bf16[6,3,2,8,2048]{4,3,2,1,0:T(8,128)(2,1)} %history_in.1, s32[8,2048]{1,0:T(8,128)} %mode_band_in.1, bf16[2,256,1024]{2,1,0:T(8,128)(2,1)} %constant.18.clone.y_table_in, ...), custom_call_target="tpu_custom_call" | custom-call | tf_op jit(solution)/shard_map/pallas_call | solution.py:493
  70.2 0.0 copy-done
  70.2 0.0 copy-done.1
  70.2 0.0 copy-start.2
  70.2 0.9 %copy-done.2 = f32[3,8,2048]{2,1,0:T(8,128)S(1)} copy-done((f32[3,8,2048]{2,1,0:T(8,128)S(1)}, f32[3,8,2048]{2,1,0:T(8,128)}, u32[]{:S(2)}) %copy-start.2) | copy-done | bytes 196632
  71.1 0.9 %shard_map.168 = (f32[3,8,2048]{2,1,0:T(8,128)}, f32[3,8,2048]{2,1,0:T(8,128)}) custom-call(f32[3,8,2048]{2,1,0:T(8,128)S(1)} %copy-done.2, f32[3,8,2048]{2,1,0:T(8,128)S(1)} %copy-done.1, f32[3,8,2048]{2,1,0:T(8,128)S(1)} %copy-done), custom_call_target="tpu_custom_call" | custom-call | tf_op jit(solution)/shard_map/pallas_call | solution.py:516
Async XLA Ops:
  0.6 69.5 %copy-start = (f32[3,8,2048]{2,1,0:T(8,128)S(1)}, f32[3,8,2048]{2,1,0:T(8,128)}, u32[]{:S(2)}) copy-start(f32[3,8,2048]{2,1,0:T(8,128)} %slip_rate.1) | copy-start | bytes 589828
  0.6 69.5 %copy-start.1 = (f32[3,8,2048]{2,1,0:T(8,128)S(1)}, f32[3,8,2048]{2,1,0:T(8,128)}, u32[]{:S(2)}) copy-start(f32[3,8,2048]{2,1,0:T(8,128)} %slip_field.1) | copy-start | bytes 589828
  70.2 0.9 %copy-start.2 = (f32[3,8,2048]{2,1,0:T(8,128)S(1)}, f32[3,8,2048]{2,1,0:T(8,128)}, u32[]{:S(2)}) copy-start(f32[3,8,2048]{2,1,0:T(8,128)} %shard_map.167.stress) | copy-start | bytes 589828

commit v4 on v3

--- a/solution.py
+++ b/solution.py
@@ -224,7 +224,7 @@
             one(lax.rem(me + 128 - step, DEV))
             return carry
 
-        lax.fori_loop(2, 128, two, 0, unroll=7)
+        lax.fori_loop(2, 128, two, 0, unroll=14)
         if forward:
             source, target = send[turn_at].at[mine], recv[turn_at].at[me]
         else:
@@ -284,10 +284,8 @@
         re = recv[turn_at][:, 0, :].T
         im = recv[turn_at][:, 1, :].T
         if turn_at == 1:
-            arrive(4)
-            rest = recv[4][:, 0, :].T
-            kept[0] = swap(jnp.concatenate([rest[0:64], re[120:128]], 0))
-            kept[1] = swap(jnp.concatenate([rest[64:128], im[120:128]], 0))
+            kept[0, 64:72] = swap(re[120:128])
+            kept[1, 64:72] = swap(im[120:128])
         re = halves(jnp.concatenate([re[:24], re[24:96] + kept[0], re[96:]], 0))
         im = halves(jnp.concatenate([im[:24], im[24:96] + kept[1], im[96:]], 0))
 
@@ -453,6 +451,10 @@
     re, im = x_inverse(now_re * now_weight, now_im * now_weight)
     hold[0] = re + hold[0]
     hold[1] = im + hold[1]
+    arrive(4)
+    rest = recv[4][:, 0, :].T
+    kept[0, 0:64] = swap(rest[0:64])
+    kept[1, 0:64] = swap(rest[64:128])
     arrive(1)
     field = y_inverse(1)
     stress = [prestress[comp] + jnp.concatenate(field[comp], 1) for comp in range(3)]

time: 72.2 us -> 72 us (level)
  no operation moved by 1% of the time
where the time goes in v4:
time: 72 us; the launch traced here: 71.9 us
  Pallas kernels  70.3 us (98%)
  local copies, waits for them, and re-layouts  0.93 us (1%)
    pallas_call x1, Pallas kernels, on_device(): pl.pallas_call(body, out_shape=shape, in_specs=[anywhere] * (5 + len(cons...  69.3 us

profile of v4, /device:TPU:1, one launch (start us, length us, event | category | flops | bytes accessed | tf_op | source)
XLA Modules:
  0.0 71.9 jit_solution(5423749800354237917)
XLA Ops:
  0.6 0.0 copy-start
  0.6 0.0 copy-start.1
  0.7 69.3 %shard_map.167.stress = f32[3,8,2048]{2,1,0:T(8,128)} custom-call(f32[3,8,2048]{2,1,0:T(8,128)} %slip_rate.1, f32[3,8,2048]{2,1,0:T(8,128)} %slip_field.1, f32[3,8,2048]{2,1,0:T(8,128)} %prestress_in.1, bf16[6,3,2,8,2048]{4,3,2,1,0:T(8,128)(2,1)} %history_in.1, s32[8,2048]{1,0:T(8,128)} %mode_band_in.1, bf16[2,256,1024]{2,1,0:T(8,128)(2,1)} %constant.18.clone.y_table_in, ...), custom_call_target="tpu_custom_call" | custom-call | tf_op jit(solution)/shard_map/pallas_call | solution.py:495
  70.0 0.0 copy-done
  70.0 0.0 copy-done.1
  70.0 0.0 copy-start.2
  70.0 0.9 %copy-done.2 = f32[3,8,2048]{2,1,0:T(8,128)S(1)} copy-done((f32[3,8,2048]{2,1,0:T(8,128)S(1)}, f32[3,8,2048]{2,1,0:T(8,128)}, u32[]{:S(2)}) %copy-start.2) | copy-done | bytes 196632
  70.9 0.9 %shard_map.168 = (f32[3,8,2048]{2,1,0:T(8,128)}, f32[3,8,2048]{2,1,0:T(8,128)}) custom-call(f32[3,8,2048]{2,1,0:T(8,128)S(1)} %copy-done.2, f32[3,8,2048]{2,1,0:T(8,128)S(1)} %copy-done.1, f32[3,8,2048]{2,1,0:T(8,128)S(1)} %copy-done), custom_call_target="tpu_custom_call" | custom-call | tf_op jit(solution)/shard_map/pallas_call | solution.py:518
Async XLA Ops:
  0.6 69.4 %copy-start = (f32[3,8,2048]{2,1,0:T(8,128)S(1)}, f32[3,8,2048]{2,1,0:T(8,128)}, u32[]{:S(2)}) copy-start(f32[3,8,2048]{2,1,0:T(8,128)} %slip_rate.1) | copy-start | bytes 589828
  0.6 69.4 %copy-start.1 = (f32[3,8,2048]{2,1,0:T(8,128)S(1)}, f32[3,8,2048]{2,1,0:T(8,128)}, u32[]{:S(2)}) copy-start(f32[3,8,2048]{2,1,0:T(8,128)} %slip_field.1) | copy-start | bytes 589828
  70.0 0.9 %copy-start.2 = (f32[3,8,2048]{2,1,0:T(8,128)S(1)}, f32[3,8,2048]{2,1,0:T(8,128)}, u32[]{:S(2)}) copy-start(f32[3,8,2048]{2,1,0:T(8,128)} %shard_map.167.stress) | copy-start | bytes 589828
